TPU v7x, 32 devices: a whole 2x2x4 slice. The times are simulated.
32 devices in a mesh: groups: 1, orient: 8 (over z, core), cls: 4 (over y, x).
Axes of the slice: x: 2, y: 2, z: 4, core: 2. Of those that a mesh axis runs over, the one named last changes fastest.
Arguments:
- particles: bfloat16 [384, 33024], P(('groups', 'orient', 'cls')), may hold values from -300 to 300
- projections: bfloat16 [8, 8, 33024], P('cls', 'orient')
- ctf: bfloat16 [8, 16512], replicated, may hold values from -1 to 1
- defocus_group: int32 [384], P(('groups', 'orient', 'cls')), may hold values from 0 to 7
- offsets: int32 [384, 2], P(('groups', 'orient', 'cls')), may hold values from -8 to 8
- routes: int32 [384, 4], P(('groups', 'orient', 'cls')), may hold values from 0 to 7, all different within a row; in each aligned block of 12 rows (0 to 11, 12 to 23, ...) at most 6 rows name the same one
Outputs:
- log_evidence: float32 [384], P(('groups', 'orient', 'cls'))
- data_sum: bfloat16 [8, 8, 33024], P(('groups', 'cls'), 'orient')
Inputs may be any that keep to these rules, and one draw needn't show every extreme that they name: `routes`: the 4 blocks of a particle differ; among the particles of one device no block is listed more than 6 times, and some block is listed exactly 6 times.
All inputs are finite; a program needn't handle non-finite values.
Results may differ from a plain program's by a relative error of at most 0.01.
The roundings to bfloat16 on the way count: a program that leaves them out, or rounds other values in their place, can miss the bound.
Values may be sent and summed in bfloat16 or wider, within the bound.
No kernel may reach another device: no remote copies, remote signals or barrier semaphores. Data moves between devices by JAX's collectives and lax.ppermute only.
A program may use at most 64 MiB of HBM per device.

v0:
```python
import math
import jax
import jax.numpy as jnp
import numpy as np
from jax import lax
from jax.sharding import PartitionSpec as P

KX = 86
KY = 192
BOX = 256
two_pi = 2.0 * math.pi
highest = lax.Precision.HIGHEST
local_across = np.array([0, 1, -1, 0, 0], dtype=np.int32)
local_down = np.array([0, 0, 0, 1, -1], dtype=np.int32)


def frequencies():
    column = jnp.arange(KX * KY, dtype=jnp.int32)
    return (column // KY, column % KY - KY // 2)


def rotation(shift_across, shift_down, freq_across, freq_down):
    turns = jnp.mod(freq_across * shift_across + freq_down * shift_down, BOX)
    angle = turns.astype(jnp.float32) * (two_pi / BOX)
    return (jnp.cos(angle), jnp.sin(angle))


def combine_stats(peaks, masses):
    top_value = jnp.max(peaks, axis=-1, keepdims=True)
    return top_value[..., 0] + jnp.log(jnp.sum(masses * jnp.exp(peaks - top_value), axis=-1))


def align_images(images, ctf_rows, shifts, freq_across, freq_down, pixel_count):
    real_part = images[:, :pixel_count].astype(jnp.float32)
    imag_part = images[:, pixel_count:].astype(jnp.float32)
    cos_base, sin_base = rotation(
        shifts[:, 0:1], shifts[:, 1:2], freq_across[None, :], freq_down[None, :]
    )
    first = (real_part * cos_base + imag_part * sin_base) * ctf_rows
    second = (imag_part * cos_base - real_part * sin_base) * ctf_rows
    return jnp.concatenate([first, second], axis=1).astype(jnp.bfloat16)


def spread_phase(table, ndim_rest):
    return table.reshape((table.shape[0],) + (1,) * ndim_rest + (table.shape[1],))


def turn_refs(ref_block, cos_shift, sin_shift, pixel_count):
    real_ref = ref_block[..., :pixel_count].astype(jnp.float32)
    imag_ref = ref_block[..., pixel_count:].astype(jnp.float32)
    cos_wide = spread_phase(cos_shift, real_ref.ndim - 1)
    sin_wide = spread_phase(sin_shift, real_ref.ndim - 1)
    first = real_ref[None] * cos_wide - imag_ref[None] * sin_wide
    second = real_ref[None] * sin_wide + imag_ref[None] * cos_wide
    turned = jnp.concatenate([first, second], axis=-1).astype(jnp.bfloat16)
    return (turned, real_ref * real_ref + imag_ref * imag_ref)


def back_rotate(summed, cos_shift, sin_shift, pixel_count):
    cos_wide = spread_phase(cos_shift, summed.ndim - 2)
    sin_wide = spread_phase(sin_shift, summed.ndim - 2)
    real_sum = summed[..., :pixel_count]
    imag_sum = summed[..., pixel_count:]
    first = jnp.sum(real_sum * cos_wide + imag_sum * sin_wide, axis=0)
    second = jnp.sum(imag_sum * cos_wide - real_sum * sin_wide, axis=0)
    return jnp.concatenate([first, second], axis=-1)


def slot_places(route_rows, orient_size):
    targets = route_rows.reshape(-1)
    onehot = (targets[:, None] == jnp.arange(orient_size, dtype=jnp.int32)[None, :]).astype(
        jnp.int32
    )
    before = jnp.cumsum(onehot, axis=0) - onehot
    return (targets, jnp.sum(before * onehot, axis=1))


def per_device(particles, projections, ctf, defocus_group, offsets, routes):
    pixel_count = KX * KY
    own_count = particles.shape[0]
    route_count = routes.shape[1]
    class_local = projections.shape[0]
    directions = projections.shape[1]
    group_count = ctf.shape[0]
    orient_size = lax.axis_size("orient")
    capacity = max(2, (own_count * route_count + orient_size - 1) // orient_size)
    total_slots = orient_size * capacity
    freq_across, freq_down = frequencies()
    ctf_table = ctf.astype(jnp.float32)
    group_onehot = (
        defocus_group[:, None] == jnp.arange(group_count, dtype=jnp.int32)[None, :]
    ).astype(jnp.float32)
    ctf_rows = jnp.dot(group_onehot, ctf_table, precision=highest)
    aligned = align_images(particles, ctf_rows, offsets, freq_across, freq_down, pixel_count)
    targets, orders = slot_places(routes, orient_size)
    slot_ids = targets * capacity + orders
    matches = (slot_ids[None, :] == jnp.arange(total_slots, dtype=jnp.int32)[:, None]).astype(
        jnp.int32
    )
    picked = jnp.sum(matches.reshape(total_slots, own_count, route_count), axis=2)
    send_images = jnp.dot(picked.astype(jnp.bfloat16), aligned, preferred_element_type=jnp.float32)
    send_images = send_images.astype(jnp.bfloat16).reshape(orient_size, capacity, 2 * pixel_count)
    send_codes = jnp.sum(picked * (defocus_group + 1)[None, :], axis=1).reshape(
        orient_size, capacity
    )
    tiles, codes = (
        lax.all_to_all(send_images, "orient", split_axis=0, concat_axis=0, tiled=True),
        lax.all_to_all(send_codes, "orient", split_axis=0, concat_axis=0, tiled=True),
    )
    rows_in = tiles.reshape(total_slots, 2 * pixel_count)
    codes_in = codes.reshape(total_slots)
    slot_groups = (
        codes_in[:, None] - 1 == jnp.arange(group_count, dtype=jnp.int32)[None, :]
    ).astype(jnp.float32)
    occupied = codes_in > 0
    cos_shift, sin_shift = rotation(
        jnp.asarray(local_across, dtype=jnp.int32)[:, None],
        jnp.asarray(local_down, dtype=jnp.int32)[:, None],
        freq_across[None, :],
        freq_down[None, :],
    )
    shift_total = cos_shift.shape[0]
    ctf_square = ctf_table * ctf_table
    ref_piece = lax.all_gather(projections, "cls", axis=0, tiled=True)
    piece_rows = ref_piece.shape[0]
    group_size = 2
    grouped = ref_piece.reshape(piece_rows // group_size, group_size, directions, 2 * pixel_count)

    def one_group(ref_block):
        turned, magnitude = turn_refs(ref_block, cos_shift, sin_shift, pixel_count)
        products = lax.dot_general(
            rows_in,
            turned.reshape(-1, 2 * pixel_count),
            (((1,), (1,)), ((), ())),
            preferred_element_type=jnp.float32,
        )
        energy = lax.dot_general(
            ctf_square,
            magnitude.reshape(group_size * directions, pixel_count),
            (((1,), (1,)), ((), ())),
            precision=highest,
        )
        slot_energy = jnp.dot(slot_groups, energy, precision=highest).reshape(
            total_slots, 1, group_size, directions
        )
        return (
            products.reshape(total_slots, shift_total, group_size, directions) - 0.5 * slot_energy
        )

    stacked = lax.map(one_group, grouped)
    scores = jnp.transpose(stacked, (1, 2, 0, 3, 4)).reshape(
        total_slots, shift_total, piece_rows, directions
    )
    slot_peak = jnp.max(scores, axis=(1, 2, 3))
    slot_mass = jnp.sum(jnp.exp(scores - slot_peak[:, None, None, None]), axis=(1, 2, 3))
    back_peak, back_mass = (
        lax.all_to_all(
            slot_peak.reshape(orient_size, capacity),
            "orient",
            split_axis=0,
            concat_axis=0,
            tiled=True,
        ),
        lax.all_to_all(
            slot_mass.reshape(orient_size, capacity),
            "orient",
            split_axis=0,
            concat_axis=0,
            tiled=True,
        ),
    )
    match_table = matches.astype(jnp.float32)
    entry_peak = jnp.dot(back_peak.reshape(-1), match_table, precision=highest).reshape(
        own_count, route_count
    )
    entry_mass = jnp.dot(back_mass.reshape(-1), match_table, precision=highest).reshape(
        own_count, route_count
    )
    log_evidence = combine_stats(entry_peak, entry_mass)
    slot_value = jnp.dot(picked.astype(jnp.float32), log_evidence, precision=highest).reshape(
        orient_size, capacity
    )
    evidence_in = lax.all_to_all(
        slot_value, "orient", split_axis=0, concat_axis=0, tiled=True
    ).reshape(total_slots)
    live = occupied[:, None, None, None]
    exponent = jnp.where(live, scores - evidence_in[:, None, None, None], 0.0)
    weights = jnp.where(live, jnp.exp(exponent), 0.0).astype(jnp.bfloat16)
    class_group_size = 2

    def one_group(group_index):
        weight_part = lax.dynamic_slice_in_dim(
            weights, group_index * class_group_size, class_group_size, 2
        )
        summed = lax.dot_general(
            weight_part.reshape(total_slots, -1),
            rows_in,
            (((0,), (0,)), ((), ())),
            preferred_element_type=jnp.float32,
        )
        summed = summed.reshape(shift_total, class_group_size, directions, 2 * pixel_count)
        return back_rotate(summed, cos_shift, sin_shift, pixel_count)

    results = lax.map(
        one_group,
        jnp.arange(class_local * lax.axis_size("cls") // class_group_size, dtype=jnp.int32),
    )
    data_sum = lax.psum_scatter(
        results.reshape(class_local * lax.axis_size("cls"), directions, 2 * pixel_count).astype(
            jnp.bfloat16
        ),
        "cls",
        scatter_dimension=0,
        tiled=True,
    )
    return (log_evidence, data_sum)


def solution(mesh):
    placed = (
        P(("groups", "orient", "cls"), None),
        P("cls", "orient", None),
        P(),
        P(("groups", "orient", "cls")),
        P(("groups", "orient", "cls"), None),
        P(("groups", "orient", "cls"), None),
    )
    return jax.shard_map(
        per_device,
        mesh=mesh,
        in_specs=placed,
        out_specs=(P(("groups", "orient", "cls")), P(("groups", "cls"), "orient", None)),
        check_vma=False,
    )
```

profile of v0, /device:TPU:0, one launch (start us, length us, event | category | flops | bytes accessed | tf_op | source)
XLA Modules:
  0.0 305.0 jit_solution(8616529737925251293)
XLA Ops:
  7.2 0.8 copy.40
  10.0 6.4 %all-to-all-start.1 = ((s32[8,1,6]{2,1,0:T(1,128)}), s32[8,1,6]{2,1,0:T(1,128)S(1)}, u32[]{:S(2)}, u32[]{:S(2)}) async-start(s32[8,1,6]{2,1,0:T(1,128)} %bitcast.3), calls=%async_computation.1 | async-start | bytes 8192 | tf_op jit(solution)/shard_map/all_to_all | solution.py:108
  17.8 6.1 %fusion.38 = (bf16[12,16512]{1,0:T(8,128)(2,1)S(1)}, bf16[12,16512]{1,0:T(8,128)(2,1)S(1)}) fusion(s32[12]{0:T(128)S(1)} %get-tuple-element.313, s32[16512]{0:T(1024)} %get-tuple-element.493, s32[12]{0:T(128)S(1)} %get-tuple-element.312, s32[16512]{0:T(1024)} %get-tuple-element.491, bf16[12,33024]{1,0:T(8,128)(2,1)} %param.12, bf16[8,16512]{1,0:T(8,128)(2,1)} %param.14, ...), kind=kOutput, calls=%fused_computation.63 | convolution fusion | flops 8718432 | bytes 1981584 | tf_op jit(solution)/shard_map/dot_general | solution.py:93
  23.9 1.0 convolution_convert_fusion
  24.9 2.6 reshape.281
  27.5 5.2 %all-to-all-start = ((bf16[8,6,33024]{2,1,0:T(8,128)(2,1)}), bf16[8,6,33024]{2,1,0:T(8,128)(2,1)}, u32[]{:S(2)}, u32[]{:S(2)}) async-start(bf16[8,6,33024]{2,1,0:T(8,128)(2,1)} %reshape.281), calls=%async_computation | async-start | bytes 8454144 | tf_op jit(solution)/shard_map/all_to_all | solution.py:107
  33.0 15.3 %all_gather.3 = bf16[8,1,33024]{2,1,0:T(2,128)(2,1)S(1)} all-gather(bf16[2,1,33024]{2,1,0:T(2,128)(2,1)S(1)} %copy.39), channel_id=1, replica_groups=mesh['groups'=1,'orient'=8,'cls'=4] {'cls'}, dimensions={0}, use_global_device_ids=true | all-gather | bytes 660480 | tf_op jit(solution)/shard_map/all_gather | solution.py:124
  48.2 3.2 %reduce.6 = bf16[8,33024]{1,0:T(8,128)(2,1)S(1)} reduce(bf16[8,1,33024]{2,1,0:T(2,128)(2,1)S(1)} %all_gather.3, bf16[]{:T(256)} %constant.106), dimensions={1}, to_apply=%all_gather.3.reduce_sub_computation | reduce | bytes 1056770 | tf_op jit(solution)/shard_map/all_gather | solution.py:124
  51.4 1.0 reshape.280
  52.4 0.9 convert_multiply_fusion.7
  53.4 74.1 %all-to-all-done = bf16[8,6,33024]{2,1,0:T(8,128)(2,1)} async-done(((bf16[8,6,33024]{2,1,0:T(8,128)(2,1)}), bf16[8,6,33024]{2,1,0:T(8,128)(2,1)}, u32[]{:S(2)}, u32[]{:S(2)}) %all-to-all-start) | async-done | bytes 3170336 | tf_op jit(solution)/shard_map/all_to_all | solution.py:107
  127.5 2.8 reshape.282
  130.4 57.9 %while.24 = (s32[]{:T(128)}, f32[4,48,5,2,1]{1,3,2,4,0:T(2,128)S(1)}, bf16[4,2,1,33024]{3,1,2,0:T(2,128)(2,1)}, bf16[48,33024]{1,0:T(8,128)(2,1)S(1)}, f32[8,165...) while((s32[]{:T(128)}, ...), condition=%wide.region_5.6_spmd.clone.clone, body=%wide.region_4.5_spmd.clone.clone.sunk | while | flops 39077952 | bytes 9925141 | solution.py:150
  130.4 3.1 %fusion.95 = (f32[5,16512]{1,0:T(8,128)S(1)}, f32[5,16512]{1,0:T(8,128)S(1)}) fusion(s32[5]{0:T(128)S(1)} %get-tuple-element.481, s32[16512]{0:T(1024)} %get-tuple-element.482, s32[5]{0:T(128)S(1)} %get-tuple-element.479, s32[16512]{0:T(1024)} %get-tuple-element.480), kind=kLoop, calls=%fused_computation.20.clone.1 | loop fusion | flops 1320960 | bytes 792616 | tf_op jit(solution)/shard_map/cos | solution.py:25
  133.5 1.0 dynamic-slice_bitcast_fusion.2
  135.1 1.4 subtract_convert_fusion.2
  136.5 2.3 add.652
  138.8 1.3 sub.142
  140.1 2.1 convolution_bitcast_fusion.5
  142.3 2.3 fusion.96
  144.9 3.1 %fusion.95 = (f32[5,16512]{1,0:T(8,128)S(1)}, f32[5,16512]{1,0:T(8,128)S(1)}) fusion(s32[5]{0:T(128)S(1)} %get-tuple-element.481, s32[16512]{0:T(1024)} %get-tuple-element.482, s32[5]{0:T(128)S(1)} %get-tuple-element.479, s32[16512]{0:T(1024)} %get-tuple-element.480), kind=kLoop, calls=%fused_computation.20.clone.1 | loop fusion | flops 1320960 | bytes 792616 | tf_op jit(solution)/shard_map/cos | solution.py:25
  148.0 1.0 dynamic-slice_bitcast_fusion.2
  149.6 1.4 subtract_convert_fusion.2
  151.0 2.3 add.652
  153.3 1.3 sub.142
  154.6 2.1 convolution_bitcast_fusion.5
  156.8 2.3 fusion.96
  159.4 3.1 %fusion.95 = (f32[5,16512]{1,0:T(8,128)S(1)}, f32[5,16512]{1,0:T(8,128)S(1)}) fusion(s32[5]{0:T(128)S(1)} %get-tuple-element.481, s32[16512]{0:T(1024)} %get-tuple-element.482, s32[5]{0:T(128)S(1)} %get-tuple-element.479, s32[16512]{0:T(1024)} %get-tuple-element.480), kind=kLoop, calls=%fused_computation.20.clone.1 | loop fusion | flops 1320960 | bytes 792616 | tf_op jit(solution)/shard_map/cos | solution.py:25
  162.4 1.0 dynamic-slice_bitcast_fusion.2
  164.1 1.4 subtract_convert_fusion.2
  165.5 2.3 add.652
  167.8 1.3 sub.142
  169.1 2.1 convolution_bitcast_fusion.5
  171.3 2.3 fusion.96
  173.8 3.1 %fusion.95 = (f32[5,16512]{1,0:T(8,128)S(1)}, f32[5,16512]{1,0:T(8,128)S(1)}) fusion(s32[5]{0:T(128)S(1)} %get-tuple-element.481, s32[16512]{0:T(1024)} %get-tuple-element.482, s32[5]{0:T(128)S(1)} %get-tuple-element.479, s32[16512]{0:T(1024)} %get-tuple-element.480), kind=kLoop, calls=%fused_computation.20.clone.1 | loop fusion | flops 1320960 | bytes 792616 | tf_op jit(solution)/shard_map/cos | solution.py:25
  176.9 1.0 dynamic-slice_bitcast_fusion.2
  178.6 1.4 subtract_convert_fusion.2
  180.0 2.3 add.652
  182.3 1.3 sub.142
  183.6 2.1 convolution_bitcast_fusion.5
  185.8 2.3 fusion.96
  189.1 3.3 %all-to-all-start.3 = ((f32[8,1,6]{2,1,0:T(1,128)}), f32[8,1,6]{2,1,0:T(1,128)S(1)}, u32[]{:S(2)}, u32[]{:S(2)}) async-start(f32[8,1,6]{2,1,0:T(1,128)} %bitcast.8), calls=%async_computation.3 | async-start | bytes 8192 | tf_op jit(solution)/shard_map/all_to_all | solution.py:164
  193.2 4.7 %all-to-all-done.3 = f32[8,1,6]{2,1,0:T(1,128)S(1)} async-done(((f32[8,1,6]{2,1,0:T(1,128)}), f32[8,1,6]{2,1,0:T(1,128)S(1)}, u32[]{:S(2)}, u32[]{:S(2)}) %all-to-all-start.3) | async-done | bytes 224 | tf_op jit(solution)/shard_map/all_to_all | solution.py:164
  197.9 3.3 %all-to-all-start.2 = ((f32[8,1,6]{2,1,0:T(1,128)}), f32[8,1,6]{2,1,0:T(1,128)S(1)}, u32[]{:S(2)}, u32[]{:S(2)}) async-start(f32[8,1,6]{2,1,0:T(1,128)} %bitcast.4), calls=%async_computation.2 | async-start | bytes 8192 | tf_op jit(solution)/shard_map/all_to_all | solution.py:157
  202.5 4.2 %all-to-all-done.2 = f32[8,1,6]{2,1,0:T(1,128)S(1)} async-done(((f32[8,1,6]{2,1,0:T(1,128)}), f32[8,1,6]{2,1,0:T(1,128)S(1)}, u32[]{:S(2)}, u32[]{:S(2)}) %all-to-all-start.2) | async-done | bytes 224 | tf_op jit(solution)/shard_map/all_to_all | solution.py:157
  209.0 3.3 %all-to-all-start.4 = ((f32[8,1,6]{2,1,0:T(1,128)}), f32[8,1,6]{2,1,0:T(1,128)S(1)}, u32[]{:S(2)}, u32[]{:S(2)}) async-start(f32[8,1,6]{2,1,0:T(1,128)} %bitcast.13), calls=%async_computation.4 | async-start | bytes 8192 | tf_op jit(solution)/shard_map/all_to_all | solution.py:183
  212.7 5.0 %all-to-all-done.4 = f32[8,1,6]{2,1,0:T(1,128)S(1)} async-done(((f32[8,1,6]{2,1,0:T(1,128)}), f32[8,1,6]{2,1,0:T(1,128)S(1)}, u32[]{:S(2)}, u32[]{:S(2)}) %all-to-all-start.4) | async-done | bytes 224 | tf_op jit(solution)/shard_map/all_to_all | solution.py:183
  218.6 28.0 %while.25 = (s32[]{:T(128)}, bf16[4,2,1,33024]{3,2,1,0:T(2,128)(2,1)}, s32[4]{0:T(128)S(1)}, bf16[48,5,8,1]{0,2,1,3:T(8,128)(2,1)S(1)}, bf16[48,33024]{1,0:T(8,1...) while((s32[]{:T(128)}, ...), condition=%wide.region_13.14_spmd.clone.clone, body=%wide.region_10.13_spmd.clone.clone.sunk | while | flops 34543108 | bytes 8065315 | solution.py:204
  220.4 3.1 %fusion.100 = (f32[5,16512]{1,0:T(8,128)S(1)}, f32[5,16512]{1,0:T(8,128)S(1)}) fusion(s32[5]{0:T(128)S(1)} %get-tuple-element.518, s32[16512]{0:T(1024)} %get-tuple-element.519, s32[5]{0:T(128)S(1)} %get-tuple-element.516, s32[16512]{0:T(1024)} %get-tuple-element.517), kind=kLoop, calls=%fused_computation.47.clone.1 | loop fusion | flops 1320960 | bytes 792616 | tf_op jit(solution)/shard_map/cos | solution.py:25
  223.5 0.9 add_reduce_fusion.3
  224.6 1.0 fusion.101
  227.4 3.1 %fusion.100 = (f32[5,16512]{1,0:T(8,128)S(1)}, f32[5,16512]{1,0:T(8,128)S(1)}) fusion(s32[5]{0:T(128)S(1)} %get-tuple-element.518, s32[16512]{0:T(1024)} %get-tuple-element.519, s32[5]{0:T(128)S(1)} %get-tuple-element.516, s32[16512]{0:T(1024)} %get-tuple-element.517), kind=kLoop, calls=%fused_computation.47.clone.1 | loop fusion | flops 1320960 | bytes 792616 | tf_op jit(solution)/shard_map/cos | solution.py:25
  230.5 0.9 add_reduce_fusion.3
  231.6 1.0 fusion.101
  234.4 3.1 %fusion.100 = (f32[5,16512]{1,0:T(8,128)S(1)}, f32[5,16512]{1,0:T(8,128)S(1)}) fusion(s32[5]{0:T(128)S(1)} %get-tuple-element.518, s32[16512]{0:T(1024)} %get-tuple-element.519, s32[5]{0:T(128)S(1)} %get-tuple-element.516, s32[16512]{0:T(1024)} %get-tuple-element.517), kind=kLoop, calls=%fused_computation.47.clone.1 | loop fusion | flops 1320960 | bytes 792616 | tf_op jit(solution)/shard_map/cos | solution.py:25
  237.5 0.9 add_reduce_fusion.3
  238.6 1.0 fusion.101
  241.4 3.1 %fusion.100 = (f32[5,16512]{1,0:T(8,128)S(1)}, f32[5,16512]{1,0:T(8,128)S(1)}) fusion(s32[5]{0:T(128)S(1)} %get-tuple-element.518, s32[16512]{0:T(1024)} %get-tuple-element.519, s32[5]{0:T(128)S(1)} %get-tuple-element.516, s32[16512]{0:T(1024)} %get-tuple-element.517), kind=kLoop, calls=%fused_computation.47.clone.1 | loop fusion | flops 1320960 | bytes 792616 | tf_op jit(solution)/shard_map/cos | solution.py:25
  244.5 0.9 add_reduce_fusion.3
  245.6 1.0 fusion.101
  246.6 4.8 %convert_reduce_fusion = bf16[4,2,33024]{2,1,0:T(2,128)(2,1)S(1)} fusion(bf16[4,2,1,33024]{3,2,1,0:T(2,128)(2,1)} %get-tuple-element.82), kind=kLoop, calls=%fused_computation.73 | loop fusion | bytes 1056768 | tf_op jit(solution)/shard_map/convert_element_type | solution.py:209
  251.4 1.0 convert_element_type.122
  253.7 42.7 %all-reduce.3.cloned.1.call-done = bf16[8,1,33024]{2,0,1:T(8,128)(2,1)} async-done(((bf16[8,1,33024]{2,0,1:T(8,128)(2,1)}), bf16[8,1,33024]{2,0,1:T(8,128)(2,1)}) %all-reduce.3.cloned.1.call-update) | async-done | bytes 528400
  296.4 1.8 constant_dynamic-slice_fusion.1
  (117 shorter events, 19.6 us)
Async XLA Ops:
  10.0 17.5 %all-to-all-start.1 = ((s32[8,1,6]{2,1,0:T(1,128)}), s32[8,1,6]{2,1,0:T(1,128)S(1)}, u32[]{:S(2)}, u32[]{:S(2)}) async-start(s32[8,1,6]{2,1,0:T(1,128)} %bitcast.3), calls=%async_computation.1 | async-start | bytes 8192 | tf_op jit(solution)/shard_map/all_to_all | solution.py:108
  27.5 5.2 %copy-start.3 = (bf16[2,1,33024]{2,0,1:T(2,128)(2,1)S(1)}, bf16[2,1,33024]{2,0,1:T(2,128)(2,1)}, u32[]{:S(2)}) copy-start(bf16[2,1,33024]{2,0,1:T(2,128)(2,1)} %param.13) | copy-start | bytes 396292
  27.5 100.0 %all-to-all-start = ((bf16[8,6,33024]{2,1,0:T(8,128)(2,1)}), bf16[8,6,33024]{2,1,0:T(8,128)(2,1)}, u32[]{:S(2)}, u32[]{:S(2)}) async-start(bf16[8,6,33024]{2,1,0:T(8,128)(2,1)} %reshape.281), calls=%async_computation | async-start | bytes 8454144 | tf_op jit(solution)/shard_map/all_to_all | solution.py:107
  48.2 4.2 %copy-start.2 = (bf16[8,16512]{1,0:T(8,128)(2,1)S(1)}, bf16[8,16512]{1,0:T(8,128)(2,1)}, u32[]{:S(2)}) copy-start(bf16[8,16512]{1,0:T(8,128)(2,1)} %param.14) | copy-start | bytes 792580
  53.4 77.0 %copy-start.4 = (s32[5]{0:T(128)S(1)}, s32[5]{0:T(128)}, u32[]{:S(2)}) copy-start(s32[5]{0:T(128)} %constant.95.clone) | copy-start | bytes 64
  53.4 77.0 %copy-start.5 = (s32[5]{0:T(128)S(1)}, s32[5]{0:T(128)}, u32[]{:S(2)}) copy-start(s32[5]{0:T(128)} %constant.96.clone) | copy-start | bytes 64
  134.5 0.7 copy-start
  140.1 2.2 copy-start.1
  149.0 0.7 copy-start
  154.6 2.2 copy-start.1
  163.5 0.7 copy-start
  169.1 2.2 copy-start.1
  177.9 0.7 copy-start
  183.6 2.2 copy-start.1
  189.1 8.9 %all-to-all-start.3 = ((f32[8,1,6]{2,1,0:T(1,128)}), f32[8,1,6]{2,1,0:T(1,128)S(1)}, u32[]{:S(2)}, u32[]{:S(2)}) async-start(f32[8,1,6]{2,1,0:T(1,128)} %bitcast.8), calls=%async_computation.3 | async-start | bytes 8192 | tf_op jit(solution)/shard_map/all_to_all | solution.py:164
  197.9 8.8 %all-to-all-start.2 = ((f32[8,1,6]{2,1,0:T(1,128)}), f32[8,1,6]{2,1,0:T(1,128)S(1)}, u32[]{:S(2)}, u32[]{:S(2)}) async-start(f32[8,1,6]{2,1,0:T(1,128)} %bitcast.4), calls=%async_computation.2 | async-start | bytes 8192 | tf_op jit(solution)/shard_map/all_to_all | solution.py:157
  208.2 10.4 %copy-start.6 = (f32[12]{0:T(128)}, f32[12]{0:T(128)S(1)}, u32[]{:S(2)}) copy-start(f32[12]{0:T(128)S(1)} %log_add_fusion) | copy-start | bytes 148
  209.0 8.8 %all-to-all-start.4 = ((f32[8,1,6]{2,1,0:T(1,128)}), f32[8,1,6]{2,1,0:T(1,128)S(1)}, u32[]{:S(2)}, u32[]{:S(2)}) async-start(f32[8,1,6]{2,1,0:T(1,128)} %bitcast.13), calls=%async_computation.4 | async-start | bytes 8192 | tf_op jit(solution)/shard_map/all_to_all | solution.py:183
  212.3 84.0 %all-reduce.3.cloned.1.call-start = ((), (), s32[]{:S(2)}) async-start(), calls=%async_computation.5 | async-start | bytes 1056768
  251.4 1.1 copy-start.7
Sparse Core Ops, SparseCore 0:
  252.5 43.7 all-reduce.2
where the time goes:
time: 307 us; the launch traced here: 305 us
  waiting for transfers between devices  131 us (43%)
  other arithmetic  46.6 us (15%)
  local copies, waits for them, and re-layouts  44 us (14%)
  matrix products  28.7 us (9%)
  starting transfers between devices  21.8 us (7%)
  blocking collectives  15.3 us (5%)
  between operations  14.9 us (5%)
    all_to_all x1, waiting for transfers between devices, per_device(): lax.all_to_all(send_images, 'orient', split_axis=0, concat_axis=0, tiled=...  74.1 us
    unnamed x2, waiting for transfers between devices  42.7 us
    cos x8, other arithmetic, rotation(): return (jnp.cos(angle), jnp.sin(angle))  24.6 us
    all_gather x1, blocking collectives, per_device(): ref_piece = lax.all_gather(projections, 'cls', axis=0, tiled=True)  15.3 us
    dot_general x4, matrix products, one_group(): lax.dot_general(ctf_square, magnitude.reshape(group_size * directions, pi...  9.16 us
    add x4, local copies, waits for them, and re-layouts, turn_refs(): second = real_ref[None] * sin_wide + imag_ref[None] * cos_wide  9.07 us
    dot_general x4, matrix products, one_group(): lax.dot_general(rows_in, turned.reshape(-1, 2 * pixel_count), (((1,), (1,...  8.57 us
    all_to_all x1, starting transfers between devices, per_device(): lax.all_to_all(send_codes, 'orient', split_axis=0, concat_axis=0, tiled=T...  6.35 us
  transfers between devices with their start and end apart: 6, of which 5 were waited for; matrix products, arithmetic and copies ran while one was open for 6% of the time, Pallas kernels for 0%

commit v1 on v0

--- a/solution.py
+++ b/solution.py
@@ -12,6 +12,19 @@
 highest = lax.Precision.HIGHEST
 local_across = np.array([0, 1, -1, 0, 0], dtype=np.int32)
 local_down = np.array([0, 0, 0, 1, -1], dtype=np.int32)
+
+
+def ring_gather(shard, axis, dim):
+    ways = lax.axis_size(axis)
+    up = [(d, (d + 1) % ways) for d in range(ways)]
+    down = [(d, (d - 1) % ways) for d in range(ways)]
+    earlier, later = ([shard], [shard])
+    for _ in range(ways // 2):
+        earlier.append(lax.ppermute(earlier[-1], axis, up))
+    for _ in range((ways - 1) // 2):
+        later.append(lax.ppermute(later[-1], axis, down))
+    line = jnp.concatenate([*earlier[::-1], *later[1:]], axis=dim)
+    return jnp.roll(line, (lax.axis_index(axis) - ways // 2) * shard.shape[dim], axis=dim)
 
 
 def frequencies():
@@ -121,7 +134,7 @@
     )
     shift_total = cos_shift.shape[0]
     ctf_square = ctf_table * ctf_table
-    ref_piece = lax.all_gather(projections, "cls", axis=0, tiled=True)
+    ref_piece = ring_gather(projections, "cls", 0)
     piece_rows = ref_piece.shape[0]
     group_size = 2
     grouped = ref_piece.reshape(piece_rows // group_size, group_size, directions, 2 * pixel_count)

time: 307 us -> 310 us (level)
  blocking collectives: 15.3 us -> 0 us
  waiting for transfers between devices: 131 us -> 144 us
  local copies, waits for them, and re-layouts: 44 us -> 49.4 us
  starting transfers between devices: 21.8 us -> 25.3 us
  other arithmetic: 46.6 us -> 43.4 us
    all_gather x1 -> x0, blocking collectives: 15.3 us -> none  [per_device(): ref_piece = lax.all_gather(projections, 'cls', axis=0, tiled=True)]
    all_to_all x1, waiting for transfers between devices: 74.1 us -> 87 us  [per_device(): lax.all_to_all(send_images, 'orient', split_axis=0, concat_axis=0, tiled=...]
    concatenate x0 -> x1, local copies, waits for them, and re-layouts: none -> 5.46 us  [ring_gather(): jnp.roll(line, (lax.axis_index(axis) - ways // 2) * shard.shape[dim], axi...]
    ppermute x0 -> x3, starting transfers between devices: none -> 4.68 us  [the longest x2 3.66 us: ring_gather(): earlier.append(lax.ppermute(earlier[-1], axis, up))]
    all_gather x1 -> x0, other arithmetic: 3.18 us -> none  [per_device(): ref_piece = lax.all_gather(projections, 'cls', axis=0, tiled=True)]
  transfers between devices with their start and end apart: 6 -> 9, of which waited for: 5 -> 6; matrix products, arithmetic and copies ran while one was open for 6% -> 7% of each run, Pallas kernels for 0% -> 0%
where the time goes in v1:
time: 310 us; the launch traced here: 308 us
  waiting for transfers between devices  144 us (46%)
  local copies, waits for them, and re-layouts  49.4 us (16%)
  other arithmetic  43.4 us (14%)
  matrix products  28.7 us (9%)
  starting transfers between devices  25.3 us (8%)
  between operations  14.9 us (5%)
    all_to_all x1, waiting for transfers between devices, per_device(): lax.all_to_all(send_images, 'orient', split_axis=0, concat_axis=0, tiled=...  87 us
    unnamed x2, waiting for transfers between devices  42.6 us
    cos x8, other arithmetic, rotation(): return (jnp.cos(angle), jnp.sin(angle))  24.6 us
    dot_general x4, matrix products, one_group(): lax.dot_general(ctf_square, magnitude.reshape(group_size * directions, pi...  9.16 us
    add x4, local copies, waits for them, and re-layouts, turn_refs(): second = real_ref[None] * sin_wide + imag_ref[None] * cos_wide  9.07 us
    dot_general x4, matrix products, one_group(): lax.dot_general(rows_in, turned.reshape(-1, 2 * pixel_count), (((1,), (1,...  8.57 us
  transfers between devices with their start and end apart: 9, of which 6 were waited for; matrix products, arithmetic and copies ran while one was open for 7% of the time, Pallas kernels for 0%

profile of v1, /device:TPU:0, one launch (start us, length us, event | category | flops | bytes accessed | tf_op | source)
XLA Modules:
  0.0 308.5 jit_solution(12903853699565778974)
XLA Ops:
  7.2 3.0 collective-permute-start
  10.2 1.0 collective-permute-start.2
  14.0 5.3 %all-to-all-start.1 = ((s32[8,1,6]{2,1,0:T(1,128)}), s32[8,1,6]{2,1,0:T(1,128)S(1)}, u32[]{:S(2)}, u32[]{:S(2)}) async-start(s32[8,1,6]{2,1,0:T(1,128)} %bitcast.3), calls=%async_computation.1 | async-start | bytes 8192 | tf_op jit(solution)/shard_map/all_to_all | solution.py:121
  20.8 6.1 %fusion.38 = (bf16[12,16512]{1,0:T(8,128)(2,1)S(1)}, bf16[12,16512]{1,0:T(8,128)(2,1)S(1)}) fusion(s32[12]{0:T(128)S(1)} %get-tuple-element.313, s32[16512]{0:T(1024)} %get-tuple-element.493, s32[12]{0:T(128)S(1)} %get-tuple-element.312, s32[16512]{0:T(1024)} %get-tuple-element.491, bf16[12,33024]{1,0:T(8,128)(2,1)} %param.12, bf16[8,16512]{1,0:T(8,128)(2,1)} %param.14, ...), kind=kOutput, calls=%fused_computation.63 | convolution fusion | flops 8718432 | bytes 1981584 | tf_op jit(solution)/shard_map/dot_general | solution.py:106
  26.9 1.0 convolution_convert_fusion
  27.9 2.6 reshape.281
  31.1 5.1 %all-to-all-start = ((bf16[8,6,33024]{2,1,0:T(8,128)(2,1)}), bf16[8,6,33024]{2,1,0:T(8,128)(2,1)}, u32[]{:S(2)}, u32[]{:S(2)}) async-start(bf16[8,6,33024]{2,1,0:T(8,128)(2,1)} %reshape.281), calls=%async_computation | async-start | bytes 8454144 | tf_op jit(solution)/shard_map/all_to_all | solution.py:120
  36.2 0.9 convert_multiply_fusion.7
  37.4 5.5 %concatenate.20 = bf16[16,1,33024]{2,0,1:T(8,128)(2,1)S(1)} concatenate(bf16[2,1,33024]{2,0,1:T(2,128)(2,1)S(1)} %collective-permute-done.1, bf16[2,1,33024]{2,0,1:T(2,128)(2,1)S(1)} %collective-permute-done, bf16[2,1,33024]{2,0,1:T(2,128)(2,1)S(1)} %copy-done.2, bf16[2,1,33024]{2,0,1:T(2,128)(2,1)S(1)} %collective-permute-done.2, ...), dimensions={0} | concatenate | bytes 2113536 | tf_op jit(solution)/shard_map/jit(_roll_dynamic)/concatenate | solution.py:27
  43.0 1.0 reshape.280
  44.1 87.0 %all-to-all-done = bf16[8,6,33024]{2,1,0:T(8,128)(2,1)} async-done(((bf16[8,6,33024]{2,1,0:T(8,128)(2,1)}), bf16[8,6,33024]{2,1,0:T(8,128)(2,1)}, u32[]{:S(2)}, u32[]{:S(2)}) %all-to-all-start) | async-done | bytes 3170336 | tf_op jit(solution)/shard_map/all_to_all | solution.py:120
  131.0 2.8 reshape.282
  133.9 57.9 %while.24 = (s32[]{:T(128)}, f32[4,48,5,2,1]{1,3,2,4,0:T(2,128)S(1)}, bf16[4,2,1,33024]{3,1,2,0:T(2,128)(2,1)}, bf16[48,33024]{1,0:T(8,128)(2,1)S(1)}, f32[8,165...) while((s32[]{:T(128)}, ...), condition=%wide.region_5.6_spmd.clone.clone, body=%wide.region_4.5_spmd.clone.clone.sunk | while | flops 39077952 | bytes 9925141 | solution.py:163
  133.9 3.1 fusion.95
  137.0 1.0 dynamic-slice_bitcast_fusion.2
  138.6 1.4 subtract_convert_fusion.2
  140.0 2.3 add.664
  142.3 1.3 sub.151
  143.6 2.1 convolution_bitcast_fusion.5
  145.8 2.3 fusion.96
  148.4 3.1 fusion.95
  151.5 1.0 dynamic-slice_bitcast_fusion.2
  153.1 1.4 subtract_convert_fusion.2
  154.5 2.3 add.664
  156.8 1.3 sub.151
  158.1 2.1 convolution_bitcast_fusion.5
  160.3 2.3 fusion.96
  162.9 3.1 fusion.95
  165.9 1.0 dynamic-slice_bitcast_fusion.2
  167.6 1.4 subtract_convert_fusion.2
  169.0 2.3 add.664
  171.3 1.3 sub.151
  172.6 2.1 convolution_bitcast_fusion.5
  174.8 2.3 fusion.96
  177.3 3.1 fusion.95
  180.4 1.0 dynamic-slice_bitcast_fusion.2
  182.1 1.4 subtract_convert_fusion.2
  183.5 2.3 add.664
  185.8 1.3 sub.151
  187.1 2.1 convolution_bitcast_fusion.5
  189.3 2.3 fusion.96
  192.6 3.3 %all-to-all-start.3 = ((f32[8,1,6]{2,1,0:T(1,128)}), f32[8,1,6]{2,1,0:T(1,128)S(1)}, u32[]{:S(2)}, u32[]{:S(2)}) async-start(f32[8,1,6]{2,1,0:T(1,128)} %bitcast.8), calls=%async_computation.3 | async-start | bytes 8192 | tf_op jit(solution)/shard_map/all_to_all | solution.py:177
  196.7 4.7 %all-to-all-done.3 = f32[8,1,6]{2,1,0:T(1,128)S(1)} async-done(((f32[8,1,6]{2,1,0:T(1,128)}), f32[8,1,6]{2,1,0:T(1,128)S(1)}, u32[]{:S(2)}, u32[]{:S(2)}) %all-to-all-start.3) | async-done | bytes 224 | tf_op jit(solution)/shard_map/all_to_all | solution.py:177
  201.4 3.3 %all-to-all-start.2 = ((f32[8,1,6]{2,1,0:T(1,128)}), f32[8,1,6]{2,1,0:T(1,128)S(1)}, u32[]{:S(2)}, u32[]{:S(2)}) async-start(f32[8,1,6]{2,1,0:T(1,128)} %bitcast.4), calls=%async_computation.2 | async-start | bytes 8192 | tf_op jit(solution)/shard_map/all_to_all | solution.py:170
  206.0 4.2 %all-to-all-done.2 = f32[8,1,6]{2,1,0:T(1,128)S(1)} async-done(((f32[8,1,6]{2,1,0:T(1,128)}), f32[8,1,6]{2,1,0:T(1,128)S(1)}, u32[]{:S(2)}, u32[]{:S(2)}) %all-to-all-start.2) | async-done | bytes 224 | tf_op jit(solution)/shard_map/all_to_all | solution.py:170
  212.5 3.3 %all-to-all-start.4 = ((f32[8,1,6]{2,1,0:T(1,128)}), f32[8,1,6]{2,1,0:T(1,128)S(1)}, u32[]{:S(2)}, u32[]{:S(2)}) async-start(f32[8,1,6]{2,1,0:T(1,128)} %bitcast.13), calls=%async_computation.4 | async-start | bytes 8192 | tf_op jit(solution)/shard_map/all_to_all | solution.py:196
  216.2 5.0 %all-to-all-done.4 = f32[8,1,6]{2,1,0:T(1,128)S(1)} async-done(((f32[8,1,6]{2,1,0:T(1,128)}), f32[8,1,6]{2,1,0:T(1,128)S(1)}, u32[]{:S(2)}, u32[]{:S(2)}) %all-to-all-start.4) | async-done | bytes 224 | tf_op jit(solution)/shard_map/all_to_all | solution.py:196
  222.1 28.0 %while.25 = (s32[]{:T(128)}, bf16[4,2,1,33024]{3,2,1,0:T(2,128)(2,1)}, s32[4]{0:T(128)S(1)}, bf16[48,5,8,1]{0,2,1,3:T(8,128)(2,1)S(1)}, bf16[48,33024]{1,0:T(8,1...) while((s32[]{:T(128)}, ...), condition=%wide.region_13.14_spmd.clone.clone, body=%wide.region_10.13_spmd.clone.clone.sunk | while | flops 34543108 | bytes 8065315 | solution.py:217
  223.9 3.1 fusion.100
  227.0 0.9 add_reduce_fusion.3
  228.1 1.0 fusion.101
  230.9 3.1 fusion.100
  234.0 0.9 add_reduce_fusion.3
  235.1 1.0 fusion.101
  237.9 3.1 fusion.100
  241.0 0.9 add_reduce_fusion.3
  242.1 1.0 fusion.101
  244.9 3.1 fusion.100
  248.0 0.9 add_reduce_fusion.3
  249.1 1.0 fusion.101
  250.1 4.8 %convert_reduce_fusion = bf16[4,2,33024]{2,1,0:T(2,128)(2,1)S(1)} fusion(bf16[4,2,1,33024]{3,2,1,0:T(2,128)(2,1)} %get-tuple-element.82), kind=kLoop, calls=%fused_computation.73 | loop fusion | bytes 1056768 | tf_op jit(solution)/shard_map/convert_element_type | solution.py:222
  254.9 1.0 convert_element_type.122
  257.2 42.6 %all-reduce.3.cloned.1.call-done = bf16[8,1,33024]{2,0,1:T(8,128)(2,1)} async-done(((bf16[8,1,33024]{2,0,1:T(8,128)(2,1)}), bf16[8,1,33024]{2,0,1:T(8,128)(2,1)}) %all-reduce.3.cloned.1.call-update) | async-done | bytes 528400
  299.8 1.8 constant_dynamic-slice_fusion.1
  (122 shorter events, 21.1 us)
Async XLA Ops:
  7.2 23.3 %collective-permute-start = (bf16[2,1,33024]{2,0,1:T(2,128)(2,1)}, bf16[2,1,33024]{2,0,1:T(2,128)(2,1)S(1)}, u32[]{:S(2)}, u32[]{:S(2)}) collective-permute-start(bf16[2,1,33024]{2,0,1:T(2,128)(2,1)} %param.13), channel_id=1, source_target_pairs={{0,1},{1,2},{2,3},{3,0},{4,5},{5,6},{6,7},{7,4},{8,9},{9,10},{10,1... | collective-permute-start | bytes 396296 | tf_op jit(solution)/shard_map/ppermute | solution.py:23
  10.2 27.0 %collective-permute-start.2 = (bf16[2,1,33024]{2,0,1:T(2,128)(2,1)}, bf16[2,1,33024]{2,0,1:T(2,128)(2,1)S(1)}, u32[]{:S(2)}, u32[]{:S(2)}) collective-permute-start(bf16[2,1,33024]{2,0,1:T(2,128)(2,1)} %param.13), channel_id=1, source_target_pairs={{0,3},{1,0},{2,1},{3,2},{4,7},{5,4},{6,5},{7,6},{8,11},{9,8},{10,9... | collective-permute-start | bytes 396296 | tf_op jit(solution)/shard_map/ppermute | solution.py:25
  14.0 17.1 %all-to-all-start.1 = ((s32[8,1,6]{2,1,0:T(1,128)}), s32[8,1,6]{2,1,0:T(1,128)S(1)}, u32[]{:S(2)}, u32[]{:S(2)}) async-start(s32[8,1,6]{2,1,0:T(1,128)} %bitcast.3), calls=%async_computation.1 | async-start | bytes 8192 | tf_op jit(solution)/shard_map/all_to_all | solution.py:121
  30.5 5.8 %copy-start.3 = (bf16[8,16512]{1,0:T(8,128)(2,1)S(1)}, bf16[8,16512]{1,0:T(8,128)(2,1)}, u32[]{:S(2)}) copy-start(bf16[8,16512]{1,0:T(8,128)(2,1)} %param.14) | copy-start | bytes 792580
  30.5 6.9 %copy-start.2 = (bf16[2,1,33024]{2,0,1:T(2,128)(2,1)S(1)}, bf16[2,1,33024]{2,0,1:T(2,128)(2,1)}, u32[]{:S(2)}) copy-start(bf16[2,1,33024]{2,0,1:T(2,128)(2,1)} %param.13) | copy-start | bytes 396292
  30.5 6.9 %collective-permute-start.1 = (bf16[2,1,33024]{2,0,1:T(2,128)(2,1)S(1)}, bf16[2,1,33024]{2,0,1:T(2,128)(2,1)S(1)}, u32[]{:S(2)}, u32[]{:S(2)}) collective-permute-start(bf16[2,1,33024]{2,0,1:T(2,128)(2,1)S(1)} %collective-permute-done), channel_id=1, source_target_pairs={{0,1},{1,2},{2,3},{3,0},{4,5},{5,6},{6,7},{7,4},{8,9},{9,10},{10,1... | collective-permute-start | bytes 396296 | tf_op jit(solution)/shard_map/ppermute | solution.py:23
  31.1 99.9 %all-to-all-start = ((bf16[8,6,33024]{2,1,0:T(8,128)(2,1)}), bf16[8,6,33024]{2,1,0:T(8,128)(2,1)}, u32[]{:S(2)}, u32[]{:S(2)}) async-start(bf16[8,6,33024]{2,1,0:T(8,128)(2,1)} %reshape.281), calls=%async_computation | async-start | bytes 8454144 | tf_op jit(solution)/shard_map/all_to_all | solution.py:120
  44.0 89.8 %copy-start.4 = (s32[5]{0:T(128)S(1)}, s32[5]{0:T(128)}, u32[]{:S(2)}) copy-start(s32[5]{0:T(128)} %constant.124.clone) | copy-start | bytes 64
  44.0 89.8 %copy-start.5 = (s32[5]{0:T(128)S(1)}, s32[5]{0:T(128)}, u32[]{:S(2)}) copy-start(s32[5]{0:T(128)} %constant.125.clone) | copy-start | bytes 64
  138.0 0.7 copy-start
  143.6 2.2 copy-start.1
  152.5 0.7 copy-start
  158.1 2.2 copy-start.1
  166.9 0.7 copy-start
  172.6 2.2 copy-start.1
  181.4 0.7 copy-start
  187.1 2.2 copy-start.1
  192.6 8.9 %all-to-all-start.3 = ((f32[8,1,6]{2,1,0:T(1,128)}), f32[8,1,6]{2,1,0:T(1,128)S(1)}, u32[]{:S(2)}, u32[]{:S(2)}) async-start(f32[8,1,6]{2,1,0:T(1,128)} %bitcast.8), calls=%async_computation.3 | async-start | bytes 8192 | tf_op jit(solution)/shard_map/all_to_all | solution.py:177
  201.4 8.8 %all-to-all-start.2 = ((f32[8,1,6]{2,1,0:T(1,128)}), f32[8,1,6]{2,1,0:T(1,128)S(1)}, u32[]{:S(2)}, u32[]{:S(2)}) async-start(f32[8,1,6]{2,1,0:T(1,128)} %bitcast.4), calls=%async_computation.2 | async-start | bytes 8192 | tf_op jit(solution)/shard_map/all_to_all | solution.py:170
  211.7 10.4 %copy-start.6 = (f32[12]{0:T(128)}, f32[12]{0:T(128)S(1)}, u32[]{:S(2)}) copy-start(f32[12]{0:T(128)S(1)} %log_add_fusion) | copy-start | bytes 148
  212.5 8.8 %all-to-all-start.4 = ((f32[8,1,6]{2,1,0:T(1,128)}), f32[8,1,6]{2,1,0:T(1,128)S(1)}, u32[]{:S(2)}, u32[]{:S(2)}) async-start(f32[8,1,6]{2,1,0:T(1,128)} %bitcast.13), calls=%async_computation.4 | async-start | bytes 8192 | tf_op jit(solution)/shard_map/all_to_all | solution.py:196
  215.8 83.9 %all-reduce.3.cloned.1.call-start = ((), (), s32[]{:S(2)}) async-start(), calls=%async_computation.5 | async-start | bytes 1056768
  254.9 1.1 copy-start.7
Sparse Core Ops, SparseCore 0:
  256.0 43.7 all-reduce.2
